TPU v7x, 32 devices: a whole 2x2x4 slice. The times are simulated.
32 devices in a mesh: parts: 2 (over y), pool: 4 (over z), tp: 4 (over x, core).
Axes of the slice: x: 2, y: 2, z: 4, core: 2. Of those that a mesh axis runs over, the one named last changes fastest.
Arguments:
- queries: bfloat16 [4096, 8192], P(('parts', 'pool'), 'tp'), parts along dimension 0, may hold values from -400 to 400
- suffix_kv: bfloat16 [2, 8, 4096, 128], P(None, 'tp', ('parts', 'pool')), parts along dimension 2, may hold values from -12 to 12
- pool_kv: bfloat16 [2, 8, 64, 128, 128], P(None, 'tp', ('parts', 'pool')), parts along dimension 2, may hold values from -6 to 6
- prefix_pages: int32 [8], P('parts'), parts along dimension 0, may hold values from 1 to 4, as said below
- owner_start: int32 [8], P('parts'), parts along dimension 0, may hold values from 0 to 3
- page_slot: int32 [8, 4, 2], P('parts'), parts along dimension 0, may hold values from 0 to 7, as said below
Outputs:
- attention: bfloat16 [4096, 8192], P(('parts', 'pool'), 'tp'), parts along dimension 0
- new_pool: bfloat16 [2, 8, 64, 128, 128], P(None, 'tp', ('parts', 'pool')), parts along dimension 2
There are 2 independent parts, one for each index of `parts`. A program takes and returns all parts, laid end to end along the dimension named above; each array names one. Nothing has to cross between parts.
Inputs may be any that keep to these rules, and one draw needn't show every extreme that they name: For each owner o, the entries page_slot[:, o, :] name each of its 8 slots exactly once. `prefix_pages`: among the 4 requests of one serving group, at least one has exactly 4 prefix pages.
All inputs are finite; a program needn't handle non-finite values.
Results may differ from a plain program's by a relative error of at most 0.0035.
Values may be sent and summed in bfloat16 or wider, within the bound.
A program may use at most 128 MiB of HBM per device.

v0:
```python
import math
import jax
import jax.numpy as jnp
from jax import lax
from jax.sharding import PartitionSpec as P


def attend_block(running, query_heads, key_rows, value_rows, visible, score_scale):
    run_max, weight_sum, accumulated = running
    scores = (
        jnp.einsum("hgqd,hkd->hgqk", query_heads, key_rows, preferred_element_type=jnp.float32)
        * score_scale
    )
    scores = jnp.where(visible, scores, -jnp.inf)
    new_max = jnp.maximum(run_max, jnp.max(scores, axis=-1))
    factor = jnp.exp(run_max - new_max)
    weights = jnp.exp(scores - new_max[..., None])
    weight_sum = weight_sum * factor + jnp.sum(weights, axis=-1)
    accumulated = accumulated * factor[..., None] + jnp.einsum(
        "hgqk,hkd->hgqd",
        weights.astype(jnp.bfloat16),
        value_rows,
        preferred_element_type=jnp.float32,
    )
    return (new_max, weight_sum, accumulated)


def attend_pages(running, query_heads, received, numbers, length, score_scale):
    page_count = received.shape[2]
    page_len = received.shape[3]
    per_block = min(page_count, max(1, 512 // page_len))
    while page_count % per_block:
        per_block = per_block - 1

    def block_step(block_index, carried):
        block_start = block_index * per_block
        block_pages = lax.dynamic_slice_in_dim(received, block_start, per_block, 2)
        key_rows = block_pages[0].reshape(
            block_pages.shape[1], per_block * page_len, block_pages.shape[4]
        )
        value_rows = block_pages[1].reshape(
            block_pages.shape[1], per_block * page_len, block_pages.shape[4]
        )
        live_pages = lax.dynamic_slice_in_dim(numbers, block_start, per_block, 0) < length
        visible = jnp.repeat(live_pages, page_len)
        return attend_block(carried, query_heads, key_rows, value_rows, visible, score_scale)

    return lax.fori_loop(0, page_count // per_block, block_step, running)


def body(queries, suffix_kv, pool_kv, prefix_pages, owner_start, page_slot):
    groups = lax.axis_size("pool")
    my_index = lax.axis_index("pool")
    local_heads = pool_kv.shape[1]
    slot_count = pool_kv.shape[2]
    page_len = pool_kv.shape[3]
    head_dim = pool_kv.shape[4]
    levels = page_slot.shape[2]
    suffix = queries.shape[0]
    per_kv = queries.shape[1] // (local_heads * head_dim)
    suffix_pages = suffix // page_len
    score_scale = 1.0 / math.sqrt(head_dim)
    length = prefix_pages[my_index]
    start_owner = owner_start[my_index]
    owners = jnp.arange(groups, dtype=jnp.int32)
    my_slots = page_slot[:, my_index, :]

    def level_rows(begin_level, end_level):
        chosen = my_slots[:, begin_level:end_level].reshape(-1)
        return jnp.take(pool_kv, chosen, axis=2)

    def numbers_of(begin_level, end_level):
        within = jnp.mod(owners - start_owner, groups)
        level_ids = jnp.arange(begin_level, end_level, dtype=jnp.int32)
        return (level_ids[None, :] * groups + within[:, None]).reshape(-1)

    own_pages = suffix_kv.reshape(2, local_heads, suffix_pages, page_len, head_dim)
    offset = jnp.mod(owners - start_owner - length, groups)
    wanted = offset < suffix_pages
    picked = jnp.take(own_pages, jnp.minimum(offset, suffix_pages - 1), axis=2)
    back_send = jnp.where(wanted[None, None, :, None, None], picked, jnp.zeros_like(picked))
    level_spans = [(level_one, level_one + 1) for level_one in range(levels)]
    first_send = level_rows(level_spans[0][0], level_spans[0][1])
    first_recv = lax.all_to_all(first_send, "pool", split_axis=2, concat_axis=2, tiled=True)
    returned = lax.all_to_all(back_send, "pool", split_axis=2, concat_axis=2, tiled=True)
    query_heads = jnp.transpose(
        queries.reshape(suffix, local_heads, per_kv, head_dim), (1, 2, 0, 3)
    )
    causal = lax.broadcasted_iota(jnp.int32, (suffix, suffix), 1) <= lax.broadcasted_iota(
        jnp.int32, (suffix, suffix), 0
    )
    running = (
        jnp.full((local_heads, per_kv, suffix), -jnp.inf, jnp.float32),
        jnp.zeros((local_heads, per_kv, suffix), jnp.float32),
        jnp.zeros((local_heads, per_kv, suffix, head_dim), jnp.float32),
    )
    running = attend_block(running, query_heads, suffix_kv[0], suffix_kv[1], causal, score_scale)
    running = attend_pages(
        running,
        query_heads,
        first_recv,
        numbers_of(level_spans[0][0], level_spans[0][1]),
        length,
        score_scale,
    )
    for begin_level, end_level in level_spans[1:]:
        later_recv = lax.all_to_all(
            level_rows(begin_level, end_level), "pool", split_axis=2, concat_axis=2, tiled=True
        )
        running = attend_pages(
            running,
            query_heads,
            later_recv,
            numbers_of(begin_level, end_level),
            length,
            score_scale,
        )
    run_max, weight_sum, accumulated = running
    result = accumulated / weight_sum[..., None]
    result = (
        jnp.transpose(result, (2, 0, 1, 3))
        .reshape(suffix, local_heads * per_kv * head_dim)
        .astype(jnp.bfloat16)
    )
    offset_in = jnp.mod(my_index - owner_start - prefix_pages, groups)
    usable = offset_in < suffix_pages
    level_ids = jnp.minimum((prefix_pages + offset_in) // groups, levels - 1)
    target = jnp.take_along_axis(my_slots, level_ids[:, None], axis=1)[:, 0]
    target = jnp.where(usable, target, slot_count)
    new_pool = pool_kv.at[:, :, target].set(returned, mode="drop")
    return (result, new_pool)


def solution(mesh):
    in_specs = (
        P(("parts", "pool"), "tp"),
        P(None, "tp", ("parts", "pool"), None),
        P(None, "tp", ("parts", "pool"), None, None),
        P("parts"),
        P("parts"),
        P("parts", None, None),
    )
    out_specs = (P(("parts", "pool"), "tp"), P(None, "tp", ("parts", "pool"), None, None))
    return jax.shard_map(body, mesh=mesh, in_specs=in_specs, out_specs=out_specs, check_vma=False)
```

profile of v0, /device:TPU:0, one launch (start us, length us, event | category | flops | bytes accessed | tf_op | source)
XLA Modules:
  0.0 122.8 jit_solution(5285862944854950834)
XLA Ops:
  0.6 1.2 %copy.61 = bf16[2,2,8,128,128]{4,3,2,1,0:T(8,128)(2,1)S(1)} copy(bf16[2,2,8,128,128]{4,3,2,1,0:T(8,128)(2,1)} %param.10) | data formatting | bytes 2097152
  3.6 6.3 %all-to-all-start = ((bf16[2,2,4,128,128]{4,3,1,0,2:T(8,128)(2,1)}), bf16[2,2,4,128,128]{4,3,1,0,2:T(8,128)(2,1)}, u32[]{:S(2)}, u32[]{:S(2)}) async-start(bf16[2,2,4,128,128]{4,3,1,0,2:T(8,128)(2,1)} %select_bitcast_fusion.1), calls=%async_computation | async-start | bytes 1048576 | tf_op jit(solution)/shard_map/all_to_all | solution.py:84
  10.0 1.3 %dynamic_slice.17 = s32[1]{0:T(128)} dynamic-slice(s32[4]{0:T(128)} %param.12, s32[]{:T(128)S(6)} %select_n.118), dynamic_slice_sizes={1} | dynamic-slice | bytes 12 | tf_op jit(solution)/shard_map/dynamic_slice | solution.py:64
  11.3 1.2 %dynamic_slice.18 = s32[1]{0:T(128)} dynamic-slice(s32[4]{0:T(128)} %param.11, s32[]{:T(128)S(6)} %select_n.118), dynamic_slice_sizes={1} | dynamic-slice | bytes 12 | tf_op jit(solution)/shard_map/dynamic_slice | solution.py:63
  13.2 1.2 fusion.50
  16.5 1.4 %gather_fusion.3 = bf16[4,2,2,128,128]{4,3,2,1,0:T(8,128)(2,1)} fusion(bf16[2,2,8,128,128]{4,3,2,1,0:T(8,128)(2,1)S(1)} %copy.61, s32[1024]{0:T(1024)S(1)} %pad_clamp_fusion.1), kind=kCustom, calls=%fused_computation.1.clone | custom fusion | bytes 1048592 | tf_op jit(solution)/shard_map/jit(_take)/gather | solution.py:70
  17.9 2.2 %copy.40 = bf16[64,8,16,128]{3,2,1,0:T(8,128)(2,1)S(1)} copy(bf16[64,8,16,128]{3,1,2,0:T(8,128)(2,1)} %bitcast.169) | data formatting | bytes 4194304
  20.1 2.5 %gather_fusion = bf16[4,2,2,128,128]{4,3,2,1,0:T(8,128)(2,1)} fusion(bf16[2,2,4,128,128]{4,3,2,1,0:T(8,128)(2,1)} %bitcast.171, s32[1024]{0:T(1024)S(1)} %pad_clamp_fusion), kind=kCustom, calls=%fused_computation.2 | custom fusion | bytes 1048592 | tf_op jit(solution)/shard_map/jit(_take)/gather | solution.py:80
  22.6 1.9 %select_bitcast_fusion = bf16[2,2,4,128,128]{4,3,1,0,2:T(8,128)(2,1)} fusion(bf16[4,2,2,128,128]{4,3,2,1,0:T(8,128)(2,1)} %gather_fusion.3, pred[4]{0:T(512)(128)(4,1)S(1)} %get-tuple-element.77), kind=kLoop, calls=%fused_computation.45 | loop fusion | flops 262144 | bytes 1048580 | tf_op jit(solution)/shard_map/jit(_take)/select_n | solution.py:70
  24.6 8.3 %fusion.2 = (f32[2,8,512]{2,1,0:T(8,128)S(1)}, f32[2,8,512,512]{2,3,1,0:T(8,128)}) fusion(pred[512,512]{0,1:T(8,128)(4,1)S(1)} %iota_compare_fusion, bf16[2,2,512,128]{3,2,1,0:T(8,128)(2,1)} %param.9, bf16[512,2,8,128]{3,2,1,0:T(8,128)(2,1)S(1)} %bitcast.166), kind=kOutput, calls=%fused_computation.15 | convolution fusion | flops 1086316544 | bytes 19431424 | tf_op jit(solution)/shard_map/hgqd,hkd->hgqk/dot_general | solution.py:11
  32.8 9.4 %fusion.3 = f32[2,8,512]{2,1,0:T(8,128)S(1)} fusion(f32[2,8,512,512]{2,3,1,0:T(8,128)} %get-tuple-element.82, f32[2,8,512]{2,1,0:T(8,128)S(1)} %get-tuple-element.81, pred[512,512]{0,1:T(8,128)(4,1)S(1)} %iota_compare_fusion), kind=kLoop, calls=%fused_computation.16 | loop fusion | flops 16769024 | bytes 17104896 | tf_op jit(solution)/shard_map/reduce_sum | solution.py:18
  42.2 5.1 %all-to-all-start.1 = ((bf16[2,2,4,128,128]{4,3,1,0,2:T(8,128)(2,1)}), bf16[2,2,4,128,128]{4,3,1,0,2:T(8,128)(2,1)}, u32[]{:S(2)}, u32[]{:S(2)}) async-start(bf16[2,2,4,128,128]{4,3,1,0,2:T(8,128)(2,1)} %select_bitcast_fusion), calls=%async_computation.1 | async-start | bytes 1048576 | tf_op jit(solution)/shard_map/all_to_all | solution.py:107
  47.4 1.2 compare_and_fusion.2
  48.6 2.0 %select_bitcast_fusion.2 = bf16[2,2,4,128,128]{4,3,1,0,2:T(8,128)(2,1)} fusion(bf16[4,2,2,128,128]{4,3,2,1,0:T(8,128)(2,1)} %gather_fusion, pred[4]{0:T(512)(128)(4,1)S(1)} %get-tuple-element.86, pred[4]{0:T(512)(128)(4,1)S(1)} %get-tuple-element.85), kind=kLoop, calls=%fused_computation.47 | loop fusion | flops 524288 | bytes 1048584 | tf_op jit(solution)/shard_map/jit(_where)/select_n | solution.py:81
  50.6 1.9 %fusion.60 = (bf16[1,2,4,128,128]{4,3,1,0,2:T(8,128)(2,1)}, bf16[1,2,4,128,128]{4,3,1,0,2:T(8,128)(2,1)}) fusion(bf16[2,2,4,128,128]{4,3,1,0,2:T(8,128)(2,1)} %all-to-all-done), kind=kLoop, calls=%fused_computation.119 | loop fusion | bytes 1048576 | tf_op jit(solution)/shard_map/while/body/eval_jaxpr/slice | solution.py:41
  52.4 1.8 %copy.24 = bf16[1,2,4,128,128]{3,2,4,1,0:T(4,128)(2,1)} copy(bf16[1,2,4,128,128]{4,3,1,0,2:T(8,128)(2,1)} %get-tuple-element.72) | data formatting | bytes 524288 | tf_op jit(solution)/shard_map/while/body/eval_jaxpr/slice | solution.py:41
  54.3 1.8 %reshape.240 = bf16[2,512,128,1]{1,2,0,3:T(8,128)(2,1)} reshape(bf16[1,2,4,128,128]{3,2,4,1,0:T(4,128)(2,1)} %copy.24) | data formatting | bytes 524288 | tf_op jit(solution)/shard_map/while/body/eval_jaxpr/reshape;while/body/eval_jaxpr/squeeze | solution.py:41
  56.0 1.7 %copy.23 = bf16[1,2,4,128,128]{4,3,2,1,0:T(8,128)(2,1)} copy(bf16[1,2,4,128,128]{4,3,1,0,2:T(8,128)(2,1)} %get-tuple-element.73) | data formatting | bytes 524288 | tf_op jit(solution)/shard_map/while/body/eval_jaxpr/slice | solution.py:38
  57.7 3.7 %all-to-all-done.1 = bf16[2,2,4,128,128]{4,3,1,0,2:T(8,128)(2,1)} async-done(((bf16[2,2,4,128,128]{4,3,1,0,2:T(8,128)(2,1)}), bf16[2,2,4,128,128]{4,3,1,0,2:T(8,128)(2,1)}, u32[]{:S(2)}, u32[]{:S(2)}) %all-to-all-start.1) | async-done | bytes 524320 | tf_op jit(solution)/shard_map/all_to_all | solution.py:107
  61.4 4.3 %all-to-all-start.2 = ((bf16[2,2,4,128,128]{4,3,1,0,2:T(8,128)(2,1)}), bf16[2,2,4,128,128]{4,3,1,0,2:T(8,128)(2,1)}, u32[]{:S(2)}, u32[]{:S(2)}) async-start(bf16[2,2,4,128,128]{4,3,1,0,2:T(8,128)(2,1)} %select_bitcast_fusion.2), calls=%async_computation.2 | async-start | bytes 1048576 | tf_op jit(solution)/shard_map/all_to_all | solution.py:85
  65.7 1.9 %fusion.61 = (bf16[1,2,4,128,128]{4,3,1,0,2:T(8,128)(2,1)}, bf16[1,2,4,128,128]{4,3,1,0,2:T(8,128)(2,1)}) fusion(bf16[2,2,4,128,128]{4,3,1,0,2:T(8,128)(2,1)} %all-to-all-done.1), kind=kLoop, calls=%fused_computation.120 | loop fusion | bytes 1048576 | tf_op jit(solution)/shard_map/while/body/eval_jaxpr/slice | solution.py:41
  67.6 1.8 %copy.27 = bf16[1,2,4,128,128]{3,2,4,1,0:T(4,128)(2,1)} copy(bf16[1,2,4,128,128]{4,3,1,0,2:T(8,128)(2,1)} %get-tuple-element.74) | data formatting | bytes 524288 | tf_op jit(solution)/shard_map/while/body/eval_jaxpr/slice | solution.py:41
  69.4 1.8 %reshape.242 = bf16[2,512,128,1]{1,2,0,3:T(8,128)(2,1)} reshape(bf16[1,2,4,128,128]{3,2,4,1,0:T(4,128)(2,1)} %copy.27) | data formatting | bytes 524288 | tf_op jit(solution)/shard_map/while/body/eval_jaxpr/reshape;while/body/eval_jaxpr/squeeze | solution.py:41
  72.2 7.7 %bitcast_reduce_fusion = (f32[2,8,512]{2,1,0:T(8,128)S(1)}, f32[2,512,8,512]{3,1,2,0:T(8,128)}) fusion(pred[512]{0:T(512)(128)(4,1)S(1)} %broadcast_bitcast_fusion, bf16[2,512,128,1]{2,1,3,0:T(8,128)(2,1)S(1)} %bitcast.173, bf16[512,2,8,128]{3,2,1,0:T(8,128)(2,1)S(1)} %bitcast.167), kind=kOutput, calls=%fused_computation.6 | convolution fusion | flops 1086316544 | bytes 19169792 | tf_op jit(solution)/shard_map/while/body/eval_jaxpr/hgqd,hkd->hgqk/dot_general | solution.py:11
  79.8 2.7 %bitcast_reduce_fusion.1 = (f32[2,8,512]{2,1,0:T(8,128)S(1)}, f32[2,512,8,512]{3,1,2,0:T(8,128)S(1)}) fusion(pred[512]{0:T(512)(128)(4,1)S(1)} %broadcast_bitcast_fusion.1, bf16[2,512,128,1]{2,1,3,0:T(8,128)(2,1)S(1)} %bitcast.172, bf16[512,2,8,128]{3,2,1,0:T(8,128)(2,1)S(1)} %bitcast.168), kind=kOutput, calls=%fused_computation.9 | convolution fusion | flops 1086316544 | bytes 19169792 | tf_op jit(solution)/shard_map/while/body/eval_jaxpr/hgqd,hkd->hgqk/dot_general | solution.py:11
  82.6 7.9 %fusion.7 = f32[2,8,512]{2,1,0:T(8,128)S(1)} fusion(f32[2,512,8,512]{3,1,2,0:T(8,128)} %get-tuple-element.80, f32[2,8,512]{2,1,0:T(8,128)S(1)} %get-tuple-element.57, pred[512]{0:T(512)(128)(4,1)S(1)} %broadcast_bitcast_fusion), kind=kLoop, calls=%fused_computation.20 | loop fusion | flops 16769024 | bytes 16843264 | tf_op jit(solution)/shard_map/while/body/eval_jaxpr/reduce_sum | solution.py:18
  90.5 8.0 %fusion.9 = f32[2,8,512,128]{2,3,1,0:T(8,128)S(1)} fusion(f32[2,512,8,512]{3,1,2,0:T(8,128)} %get-tuple-element.80, f32[2,8,512]{2,1,0:T(8,128)S(1)} %get-tuple-element.57, pred[512]{0:T(512)(128)(4,1)S(1)} %broadcast_bitcast_fusion, bf16[2,512,128,1]{1,2,0,3:T(8,128)(2,1)S(1)} %copy-done.6), kind=kOutput, calls=%fused_computation.22 | convolution fusion | flops 1090519040 | bytes 21266944 | tf_op jit(solution)/shard_map/while/body/eval_jaxpr/hgqk,hkd->hgqd/dot_general | solution.py:19
  98.5 3.8 %fusion.5 = f32[2,8,512]{2,1,0:T(8,128)S(1)} fusion(f32[2,512,8,512]{3,1,2,0:T(8,128)S(1)} %get-tuple-element.84, f32[2,8,512]{2,1,0:T(8,128)S(1)} %get-tuple-element.58, pred[512]{0:T(512)(128)(4,1)S(1)} %broadcast_bitcast_fusion.1), kind=kLoop, calls=%fused_computation.18 | loop fusion | flops 16769024 | bytes 16843264 | tf_op jit(solution)/shard_map/while/body/eval_jaxpr/reduce_sum | solution.py:18
  102.3 5.5 %fusion.11 = f32[2,8,512,128]{2,3,1,0:T(8,128)} fusion(f32[2,512,8,512]{3,1,2,0:T(8,128)S(1)} %get-tuple-element.84, f32[2,8,512]{2,1,0:T(8,128)S(1)} %get-tuple-element.58, pred[512]{0:T(512)(128)(4,1)S(1)} %broadcast_bitcast_fusion.1, bf16[2,512,128,1]{1,2,0,3:T(8,128)(2,1)S(1)} %copy-done.5), kind=kOutput, calls=%fused_computation.23 | convolution fusion | flops 1090519040 | bytes 21266944 | tf_op jit(solution)/shard_map/while/body/eval_jaxpr/hgqk,hkd->hgqd/dot_general | solution.py:19
  107.9 9.7 %fusion.19 = bf16[512,2,8,128]{0,3,2,1:T(8,128)(2,1)S(1)} fusion(f32[2,8,512,128]{2,3,1,0:T(8,128)S(1)} %fusion.9, f32[2,8,512,128]{2,3,1,0:T(8,128)} %fusion.11, f32[2,8,512,512]{2,3,1,0:T(8,128)} %get-tuple-element.82, f32[2,8,512]{2,1,0:T(8,128)S(1)} %get-tuple-element.81, pred[512,512]{0,1:T(8,128)(4,1)S(1)} %iota_compare_fusion, ...), kind=kOutput, calls=%fused_computation.30 | convolution fusion | flops 1097859072 | bytes 27951104 | tf_op jit(solution)/shard_map/hgqk,hkd->hgqd/dot_general | solution.py:19
  117.6 2.4 %copy.29 = bf16[512,2048]{1,0:T(8,128)(2,1)} copy(bf16[512,2048]{0,1:T(8,128)(2,1)S(1)} %bitcast.170) | data formatting | bytes 4194304
  120.0 1.8 %scatter_fusion = bf16[2,2,8,128,128]{4,3,2,1,0:T(8,128)(2,1)S(1)} fusion(bf16[2,2,8,128,128]{4,3,2,1,0:T(8,128)(2,1)S(1)} %copy.61, s32[4]{0:T(128)S(1)} %compare_select_fusion.4, bf16[4,2,2,128,128]{4,3,2,1,0:T(8,128)(2,1)} %bitcast.42), kind=kCustom, calls=%fused_computation.4 | custom fusion | bytes 1572880 | tf_op jit(solution)/shard_map/scatter | solution.py:130
  (37 shorter events, 6.6 us)
Async XLA Ops:
  0.6 1.3 %copy-start = (s32[4,4,2]{1,2,0:T(2,128)S(1)}, s32[4,4,2]{1,2,0:T(2,128)}, u32[]{:S(2)}) copy-start(s32[4,4,2]{1,2,0:T(2,128)} %param.13) | copy-start | bytes 388
  3.6 38.6 %all-to-all-start = ((bf16[2,2,4,128,128]{4,3,1,0,2:T(8,128)(2,1)}), bf16[2,2,4,128,128]{4,3,1,0,2:T(8,128)(2,1)}, u32[]{:S(2)}, u32[]{:S(2)}) async-start(bf16[2,2,4,128,128]{4,3,1,0,2:T(8,128)(2,1)} %select_bitcast_fusion.1), calls=%async_computation | async-start | bytes 1048576 | tf_op jit(solution)/shard_map/all_to_all | solution.py:84
  42.2 19.1 %all-to-all-start.1 = ((bf16[2,2,4,128,128]{4,3,1,0,2:T(8,128)(2,1)}), bf16[2,2,4,128,128]{4,3,1,0,2:T(8,128)(2,1)}, u32[]{:S(2)}, u32[]{:S(2)}) async-start(bf16[2,2,4,128,128]{4,3,1,0,2:T(8,128)(2,1)} %select_bitcast_fusion), calls=%async_computation.1 | async-start | bytes 1048576 | tf_op jit(solution)/shard_map/all_to_all | solution.py:107
  61.4 58.6 %all-to-all-start.2 = ((bf16[2,2,4,128,128]{4,3,1,0,2:T(8,128)(2,1)}), bf16[2,2,4,128,128]{4,3,1,0,2:T(8,128)(2,1)}, u32[]{:S(2)}, u32[]{:S(2)}) async-start(bf16[2,2,4,128,128]{4,3,1,0,2:T(8,128)(2,1)} %select_bitcast_fusion.2), calls=%async_computation.2 | async-start | bytes 1048576 | tf_op jit(solution)/shard_map/all_to_all | solution.py:85
  71.2 8.7 %copy-start.4 = (bf16[1,2,4,128,128]{4,3,2,1,0:T(8,128)(2,1)S(1)}, bf16[1,2,4,128,128]{4,3,2,1,0:T(8,128)(2,1)}, u32[]{:S(2)}) copy-start(bf16[1,2,4,128,128]{4,3,2,1,0:T(8,128)(2,1)} %copy.23) | copy-start | bytes 786436
  79.8 10.7 %copy-start.6 = (bf16[2,512,128,1]{1,2,0,3:T(8,128)(2,1)S(1)}, bf16[2,512,128,1]{1,2,0,3:T(8,128)(2,1)}, u32[]{:S(2)}) copy-start(bf16[2,512,128,1]{1,2,0,3:T(8,128)(2,1)} %reshape.242) | copy-start | bytes 786436
  90.5 11.8 %copy-start.5 = (bf16[2,512,128,1]{1,2,0,3:T(8,128)(2,1)S(1)}, bf16[2,512,128,1]{1,2,0,3:T(8,128)(2,1)}, u32[]{:S(2)}) copy-start(bf16[2,512,128,1]{1,2,0,3:T(8,128)(2,1)} %reshape.240) | copy-start | bytes 786436
  98.5 9.4 %copy-start.3 = (bf16[2,2,512,128]{3,2,1,0:T(8,128)(2,1)S(1)}, bf16[2,2,512,128]{3,2,1,0:T(8,128)(2,1)}, u32[]{:S(2)}) copy-start(bf16[2,2,512,128]{3,2,1,0:T(8,128)(2,1)} %param.9) | copy-start | bytes 1572868
  107.8 14.9 %copy-start.1 = (s32[4,4,2]{1,2,0:T(2,128)S(1)}, s32[4,4,2]{1,2,0:T(2,128)}, u32[]{:S(2)}) copy-start(s32[4,4,2]{1,2,0:T(2,128)} %param.13) | copy-start | bytes 388
  121.8 1.0 copy-start.2
where the time goes:
time: 124 us; the launch traced here: 123 us
  matrix products  41.8 us (34%)
  other arithmetic  30.5 us (25%)
  local copies, waits for them, and re-layouts  30.1 us (24%)
  starting transfers between devices  15.8 us (13%)
  waiting for transfers between devices  3.71 us (3%)
    dot_general x3, matrix products, attend_block(): jnp.einsum('hgqk,hkd->hgqd', weights.astype(jnp.bfloat16), value_rows, pr...  23.2 us
    reduce_sum x3, other arithmetic, attend_block(): weight_sum = weight_sum * factor + jnp.sum(weights, axis=-1)  21.1 us
    dot_general x3, matrix products, attend_block(): jnp.einsum('hgqd,hkd->hgqk', query_heads, key_rows, preferred_element_typ...  18.6 us
    slice x4, local copies, waits for them, and re-layouts, block_step(): block_pages[1]  7.37 us
    unnamed x18, local copies, waits for them, and re-layouts  6.81 us
    all_to_all x1, starting transfers between devices, body(): lax.all_to_all(first_send, 'pool', split_axis=2, concat_axis=2, tiled=True)  6.35 us
    all_to_all x1, starting transfers between devices, body(): lax.all_to_all(level_rows(begin_level, end_level), 'pool', split_axis=2,...  5.11 us
    all_to_all x1, starting transfers between devices, body(): lax.all_to_all(back_send, 'pool', split_axis=2, concat_axis=2, tiled=True)  4.32 us
  transfers between devices with their start and end apart: 3, of which 1 were waited for; matrix products, arithmetic and copies ran while one was open for 79% of the time, Pallas kernels for 0%

commit v1 on v0

--- a/solution.py
+++ b/solution.py
@@ -81,7 +81,12 @@
     back_send = jnp.where(wanted[None, None, :, None, None], picked, jnp.zeros_like(picked))
     level_spans = [(level_one, level_one + 1) for level_one in range(levels)]
     first_send = level_rows(level_spans[0][0], level_spans[0][1])
-    first_recv = lax.all_to_all(first_send, "pool", split_axis=2, concat_axis=2, tiled=True)
+    first_recv = jnp.concatenate(
+        lax.all_to_all(
+            jnp.stack(jnp.split(first_send, lax.axis_size("pool"), 2), axis=0), "pool", 0, 0
+        ),
+        2,
+    )
     returned = lax.all_to_all(back_send, "pool", split_axis=2, concat_axis=2, tiled=True)
     query_heads = jnp.transpose(
         queries.reshape(suffix, local_heads, per_kv, head_dim), (1, 2, 0, 3)

time: 124 us -> 124 us (level)
  no operation moved by 1% of the time
where the time goes in v1:
time: 124 us; the launch traced here: 123 us
  matrix products  41.8 us (34%)
  other arithmetic  30.7 us (25%)
  local copies, waits for them, and re-layouts  30.2 us (24%)
  starting transfers between devices  15.8 us (13%)
  waiting for transfers between devices  3.66 us (3%)
    dot_general x3, matrix products, attend_block(): jnp.einsum('hgqk,hkd->hgqd', weights.astype(jnp.bfloat16), value_rows, pr...  23.2 us
    reduce_sum x3, other arithmetic, attend_block(): weight_sum = weight_sum * factor + jnp.sum(weights, axis=-1)  21.1 us
    dot_general x3, matrix products, attend_block(): jnp.einsum('hgqd,hkd->hgqk', query_heads, key_rows, preferred_element_typ...  18.6 us
    slice x4, local copies, waits for them, and re-layouts, block_step(): block_pages[1]  7.37 us
    unnamed x18, local copies, waits for them, and re-layouts  6.81 us
    all_to_all x1, starting transfers between devices, body(): lax.all_to_all(jnp.stack(jnp.split(first_send, lax.axis_size('pool'), 2),...  6.35 us
    all_to_all x1, starting transfers between devices, body(): lax.all_to_all(level_rows(begin_level, end_level), 'pool', split_axis=2,...  5.11 us
    all_to_all x1, starting transfers between devices, body(): lax.all_to_all(back_send, 'pool', split_axis=2, concat_axis=2, tiled=True)  4.31 us
  transfers between devices with their start and end apart: 3, of which 1 were waited for; matrix products, arithmetic and copies ran while one was open for 79% of the time, Pallas kernels for 0%

profile of v1, /device:TPU:0, one launch (start us, length us, event | category | flops | bytes accessed | tf_op | source)
XLA Modules:
  0.0 123.1 jit_solution(14236600993438357906)
XLA Ops:
  3.8 6.3 %all-to-all-start = ((bf16[4,2,2,1,128,128]{5,4,2,1,3,0:T(8,128)(2,1)}), bf16[4,2,2,1,128,128]{5,4,2,1,3,0:T(8,128)(2,1)}, u32[]{:S(2)}, u32[]{:S(2)}) async-start(bf16[4,2,2,1,128,128]{5,4,2,1,3,0:T(8,128)(2,1)} %pad_maximum_fusion), calls=%async_computation | async-start | bytes 1048576 | tf_op jit(solution)/shard_map/all_to_all | solution.py:85
  10.1 1.3 %dynamic_slice.17 = s32[1]{0:T(128)} dynamic-slice(s32[4]{0:T(128)} %param.12, s32[]{:T(128)S(6)} %select_n.118), dynamic_slice_sizes={1} | dynamic-slice | bytes 12 | tf_op jit(solution)/shard_map/dynamic_slice | solution.py:64
  11.4 1.3 %dynamic_slice.18 = s32[1]{0:T(128)} dynamic-slice(s32[4]{0:T(128)} %param.11, s32[]{:T(128)S(6)} %select_n.118), dynamic_slice_sizes={1} | dynamic-slice | bytes 12 | tf_op jit(solution)/shard_map/dynamic_slice | solution.py:63
  13.4 1.3 %fusion.50 = s32[4]{0:T(128)S(1)} fusion(s32[]{:T(128)} %bitcast.10, s32[]{:T(128)} %bitcast.9), kind=kLoop, calls=%fused_computation.110 | loop fusion | flops 68 | bytes 24 | tf_op jit(solution)/shard_map/jit(_take)/jit(_where)/select_n | solution.py:80
  14.6 1.3 %add_compare_fusion = (pred[4]{0:T(512)(128)(4,1)S(1)}, pred[4]{0:T(512)(128)(4,1)S(1)}) fusion(s32[]{:T(128)} %bitcast.10, s32[]{:T(128)} %bitcast.9), kind=kLoop, calls=%fused_computation.112 | loop fusion | flops 60 | bytes 16 | tf_op jit(solution)/shard_map/while/body/eval_jaxpr/lt | solution.py:44
  16.8 1.4 %gather_fusion.3 = bf16[4,2,2,128,128]{4,3,2,1,0:T(8,128)(2,1)} fusion(bf16[2,2,8,128,128]{4,3,2,1,0:T(8,128)(2,1)S(1)} %copy.61, s32[1024]{0:T(1024)S(1)} %pad_clamp_fusion.1), kind=kCustom, calls=%fused_computation.1.clone | custom fusion | bytes 1048592 | tf_op jit(solution)/shard_map/jit(_take)/gather | solution.py:70
  18.2 2.2 %copy.40 = bf16[64,8,16,128]{3,2,1,0:T(8,128)(2,1)S(1)} copy(bf16[64,8,16,128]{3,1,2,0:T(8,128)(2,1)} %bitcast.178) | data formatting | bytes 4194304
  20.4 2.5 %gather_fusion = bf16[4,2,2,128,128]{4,3,2,1,0:T(8,128)(2,1)} fusion(bf16[2,2,4,128,128]{4,3,2,1,0:T(8,128)(2,1)} %bitcast.180, s32[1024]{0:T(1024)S(1)} %pad_clamp_fusion), kind=kCustom, calls=%fused_computation.2 | custom fusion | bytes 1048592 | tf_op jit(solution)/shard_map/jit(_take)/gather | solution.py:80
  22.9 1.9 %select_bitcast_fusion = bf16[2,2,4,128,128]{4,3,1,0,2:T(8,128)(2,1)} fusion(bf16[4,2,2,128,128]{4,3,2,1,0:T(8,128)(2,1)} %gather_fusion.3, pred[4]{0:T(512)(128)(4,1)S(1)} %get-tuple-element.81), kind=kLoop, calls=%fused_computation.46 | loop fusion | flops 262144 | bytes 1048580 | tf_op jit(solution)/shard_map/jit(_take)/select_n | solution.py:70
  24.9 8.3 %fusion.2 = (f32[2,8,512]{2,1,0:T(8,128)S(1)}, f32[2,8,512,512]{2,3,1,0:T(8,128)}) fusion(pred[512,512]{0,1:T(8,128)(4,1)S(1)} %iota_compare_fusion, bf16[2,2,512,128]{3,2,1,0:T(8,128)(2,1)} %param.9, bf16[512,2,8,128]{3,2,1,0:T(8,128)(2,1)S(1)} %bitcast.175), kind=kOutput, calls=%fused_computation.15 | convolution fusion | flops 1086316544 | bytes 19431424 | tf_op jit(solution)/shard_map/hgqd,hkd->hgqk/dot_general | solution.py:11
  33.1 9.4 %fusion.3 = f32[2,8,512]{2,1,0:T(8,128)S(1)} fusion(f32[2,8,512,512]{2,3,1,0:T(8,128)} %get-tuple-element.86, f32[2,8,512]{2,1,0:T(8,128)S(1)} %get-tuple-element.85, pred[512,512]{0,1:T(8,128)(4,1)S(1)} %iota_compare_fusion), kind=kLoop, calls=%fused_computation.16 | loop fusion | flops 16769024 | bytes 17104896 | tf_op jit(solution)/shard_map/reduce_sum | solution.py:18
  42.6 5.1 %all-to-all-start.1 = ((bf16[2,2,4,128,128]{4,3,1,0,2:T(8,128)(2,1)}), bf16[2,2,4,128,128]{4,3,1,0,2:T(8,128)(2,1)}, u32[]{:S(2)}, u32[]{:S(2)}) async-start(bf16[2,2,4,128,128]{4,3,1,0,2:T(8,128)(2,1)} %select_bitcast_fusion), calls=%async_computation.1 | async-start | bytes 1048576 | tf_op jit(solution)/shard_map/all_to_all | solution.py:112
  47.7 1.3 %compare_and_fusion.2 = (pred[4]{0:T(512)(128)(4,1)S(1)}, pred[4]{0:T(512)(128)(4,1)S(1)}) fusion(s32[]{:T(128)} %bitcast.10, s32[]{:T(128)} %bitcast.9), kind=kLoop, calls=%fused_computation.92 | loop fusion | flops 84 | bytes 16 | tf_op jit(solution)/shard_map/jit(_take)/and | solution.py:80
  49.0 2.0 %select_bitcast_fusion.2 = bf16[2,2,4,128,128]{4,3,1,0,2:T(8,128)(2,1)} fusion(bf16[4,2,2,128,128]{4,3,2,1,0:T(8,128)(2,1)} %gather_fusion, pred[4]{0:T(512)(128)(4,1)S(1)} %get-tuple-element.90, pred[4]{0:T(512)(128)(4,1)S(1)} %get-tuple-element.89), kind=kLoop, calls=%fused_computation.48 | loop fusion | flops 524288 | bytes 1048584 | tf_op jit(solution)/shard_map/jit(_where)/select_n | solution.py:81
  50.9 1.9 %fusion.60 = (bf16[1,2,4,1,128,128]{5,4,1,0,3,2:T(8,128)(2,1)}, bf16[1,2,4,1,128,128]{5,4,1,0,3,2:T(8,128)(2,1)}) fusion(bf16[2,2,4,1,128,128]{5,4,1,0,3,2:T(8,128)(2,1)} %bitcast.19), kind=kLoop, calls=%fused_computation.124 | loop fusion | bytes 1048576 | tf_op jit(solution)/shard_map/while/body/eval_jaxpr/slice | solution.py:41
  52.8 1.8 %copy.24 = bf16[1,2,4,1,128,128]{4,2,5,1,3,0:T(4,128)(2,1)} copy(bf16[1,2,4,1,128,128]{5,4,1,0,3,2:T(8,128)(2,1)} %get-tuple-element.72) | data formatting | bytes 524288 | tf_op jit(solution)/shard_map/while/body/eval_jaxpr/slice | solution.py:41
  54.6 1.8 %reshape.249 = bf16[2,512,128,1]{1,2,0,3:T(8,128)(2,1)} reshape(bf16[1,2,4,1,128,128]{4,2,5,1,3,0:T(4,128)(2,1)} %copy.24) | data formatting | bytes 524288 | tf_op jit(solution)/shard_map/while/body/eval_jaxpr/reshape;while/body/eval_jaxpr/squeeze | solution.py:41
  56.4 1.7 %copy.23 = bf16[1,2,4,1,128,128]{5,4,2,1,3,0:T(8,128)(2,1)} copy(bf16[1,2,4,1,128,128]{5,4,1,0,3,2:T(8,128)(2,1)} %get-tuple-element.73) | data formatting | bytes 524288 | tf_op jit(solution)/shard_map/while/body/eval_jaxpr/slice | solution.py:38
  58.0 3.7 %all-to-all-done.1 = bf16[2,2,4,128,128]{4,3,1,0,2:T(8,128)(2,1)} async-done(((bf16[2,2,4,128,128]{4,3,1,0,2:T(8,128)(2,1)}), bf16[2,2,4,128,128]{4,3,1,0,2:T(8,128)(2,1)}, u32[]{:S(2)}, u32[]{:S(2)}) %all-to-all-start.1) | async-done | bytes 524320 | tf_op jit(solution)/shard_map/all_to_all | solution.py:112
  61.7 4.3 %all-to-all-start.2 = ((bf16[2,2,4,128,128]{4,3,1,0,2:T(8,128)(2,1)}), bf16[2,2,4,128,128]{4,3,1,0,2:T(8,128)(2,1)}, u32[]{:S(2)}, u32[]{:S(2)}) async-start(bf16[2,2,4,128,128]{4,3,1,0,2:T(8,128)(2,1)} %select_bitcast_fusion.2), calls=%async_computation.2 | async-start | bytes 1048576 | tf_op jit(solution)/shard_map/all_to_all | solution.py:90
  66.0 1.9 %fusion.61 = (bf16[1,2,4,128,128]{4,3,1,0,2:T(8,128)(2,1)}, bf16[1,2,4,128,128]{4,3,1,0,2:T(8,128)(2,1)}) fusion(bf16[2,2,4,128,128]{4,3,1,0,2:T(8,128)(2,1)} %all-to-all-done.1), kind=kLoop, calls=%fused_computation.125 | loop fusion | bytes 1048576 | tf_op jit(solution)/shard_map/while/body/eval_jaxpr/slice | solution.py:41
  67.9 1.8 %copy.27 = bf16[1,2,4,128,128]{3,2,4,1,0:T(4,128)(2,1)} copy(bf16[1,2,4,128,128]{4,3,1,0,2:T(8,128)(2,1)} %get-tuple-element.74) | data formatting | bytes 524288 | tf_op jit(solution)/shard_map/while/body/eval_jaxpr/slice | solution.py:41
  69.7 1.8 %reshape.251 = bf16[2,512,128,1]{1,2,0,3:T(8,128)(2,1)} reshape(bf16[1,2,4,128,128]{3,2,4,1,0:T(4,128)(2,1)} %copy.27) | data formatting | bytes 524288 | tf_op jit(solution)/shard_map/while/body/eval_jaxpr/reshape;while/body/eval_jaxpr/squeeze | solution.py:41
  72.5 7.6 %bitcast_reduce_fusion = (f32[2,8,512]{2,1,0:T(8,128)S(1)}, f32[2,512,8,512]{3,1,2,0:T(8,128)}) fusion(pred[512]{0:T(512)(128)(4,1)S(1)} %broadcast_bitcast_fusion, bf16[2,512,128,1]{2,1,3,0:T(8,128)(2,1)S(1)} %bitcast.182, bf16[512,2,8,128]{3,2,1,0:T(8,128)(2,1)S(1)} %bitcast.176), kind=kOutput, calls=%fused_computation.6 | convolution fusion | flops 1086316544 | bytes 19169792 | tf_op jit(solution)/shard_map/while/body/eval_jaxpr/hgqd,hkd->hgqk/dot_general | solution.py:11
  80.1 2.7 %bitcast_reduce_fusion.1 = (f32[2,8,512]{2,1,0:T(8,128)S(1)}, f32[2,512,8,512]{3,1,2,0:T(8,128)S(1)}) fusion(pred[512]{0:T(512)(128)(4,1)S(1)} %broadcast_bitcast_fusion.1, bf16[2,512,128,1]{2,1,3,0:T(8,128)(2,1)S(1)} %bitcast.181, bf16[512,2,8,128]{3,2,1,0:T(8,128)(2,1)S(1)} %bitcast.177), kind=kOutput, calls=%fused_computation.9 | convolution fusion | flops 1086316544 | bytes 19169792 | tf_op jit(solution)/shard_map/while/body/eval_jaxpr/hgqd,hkd->hgqk/dot_general | solution.py:11
  82.9 7.9 %fusion.7 = f32[2,8,512]{2,1,0:T(8,128)S(1)} fusion(f32[2,512,8,512]{3,1,2,0:T(8,128)} %get-tuple-element.84, f32[2,8,512]{2,1,0:T(8,128)S(1)} %get-tuple-element.57, pred[512]{0:T(512)(128)(4,1)S(1)} %broadcast_bitcast_fusion), kind=kLoop, calls=%fused_computation.20 | loop fusion | flops 16769024 | bytes 16843264 | tf_op jit(solution)/shard_map/while/body/eval_jaxpr/reduce_sum | solution.py:18
  90.8 8.0 %fusion.9 = f32[2,8,512,128]{2,3,1,0:T(8,128)S(1)} fusion(f32[2,512,8,512]{3,1,2,0:T(8,128)} %get-tuple-element.84, f32[2,8,512]{2,1,0:T(8,128)S(1)} %get-tuple-element.57, pred[512]{0:T(512)(128)(4,1)S(1)} %broadcast_bitcast_fusion, bf16[2,512,128,1]{1,2,0,3:T(8,128)(2,1)S(1)} %copy-done.6), kind=kOutput, calls=%fused_computation.22 | convolution fusion | flops 1090519040 | bytes 21266944 | tf_op jit(solution)/shard_map/while/body/eval_jaxpr/hgqk,hkd->hgqd/dot_general | solution.py:19
  98.8 3.8 %fusion.5 = f32[2,8,512]{2,1,0:T(8,128)S(1)} fusion(f32[2,512,8,512]{3,1,2,0:T(8,128)S(1)} %get-tuple-element.88, f32[2,8,512]{2,1,0:T(8,128)S(1)} %get-tuple-element.58, pred[512]{0:T(512)(128)(4,1)S(1)} %broadcast_bitcast_fusion.1), kind=kLoop, calls=%fused_computation.18 | loop fusion | flops 16769024 | bytes 16843264 | tf_op jit(solution)/shard_map/while/body/eval_jaxpr/reduce_sum | solution.py:18
  102.6 5.5 %fusion.11 = f32[2,8,512,128]{2,3,1,0:T(8,128)} fusion(f32[2,512,8,512]{3,1,2,0:T(8,128)S(1)} %get-tuple-element.88, f32[2,8,512]{2,1,0:T(8,128)S(1)} %get-tuple-element.58, pred[512]{0:T(512)(128)(4,1)S(1)} %broadcast_bitcast_fusion.1, bf16[2,512,128,1]{1,2,0,3:T(8,128)(2,1)S(1)} %copy-done.5), kind=kOutput, calls=%fused_computation.23 | convolution fusion | flops 1090519040 | bytes 21266944 | tf_op jit(solution)/shard_map/while/body/eval_jaxpr/hgqk,hkd->hgqd/dot_general | solution.py:19
  108.2 9.7 %fusion.19 = bf16[512,2,8,128]{0,3,2,1:T(8,128)(2,1)S(1)} fusion(f32[2,8,512,128]{2,3,1,0:T(8,128)S(1)} %fusion.9, f32[2,8,512,128]{2,3,1,0:T(8,128)} %fusion.11, f32[2,8,512,512]{2,3,1,0:T(8,128)} %get-tuple-element.86, f32[2,8,512]{2,1,0:T(8,128)S(1)} %get-tuple-element.85, pred[512,512]{0,1:T(8,128)(4,1)S(1)} %iota_compare_fusion, ...), kind=kOutput, calls=%fused_computation.30 | convolution fusion | flops 1097859072 | bytes 27951104 | tf_op jit(solution)/shard_map/hgqk,hkd->hgqd/dot_general | solution.py:19
  117.9 2.4 %copy.29 = bf16[512,2048]{1,0:T(8,128)(2,1)} copy(bf16[512,2048]{0,1:T(8,128)(2,1)S(1)} %bitcast.179) | data formatting | bytes 4194304
  120.3 1.8 %scatter_fusion = bf16[2,2,8,128,128]{4,3,2,1,0:T(8,128)(2,1)S(1)} fusion(bf16[2,2,8,128,128]{4,3,2,1,0:T(8,128)(2,1)S(1)} %copy.61, s32[4]{0:T(128)S(1)} %compare_select_fusion.4, bf16[4,2,2,128,128]{4,3,2,1,0:T(8,128)(2,1)} %bitcast.47), kind=kCustom, calls=%fused_computation.4 | custom fusion | bytes 1572880 | tf_op jit(solution)/shard_map/scatter | solution.py:135
  (39 shorter events, 6.7 us)
Async XLA Ops:
  0.6 1.3 %copy-start = (s32[4,4,2]{1,2,0:T(2,128)S(1)}, s32[4,4,2]{1,2,0:T(2,128)}, u32[]{:S(2)}) copy-start(s32[4,4,2]{1,2,0:T(2,128)} %param.13) | copy-start | bytes 388
  3.8 38.8 %all-to-all-start = ((bf16[4,2,2,1,128,128]{5,4,2,1,3,0:T(8,128)(2,1)}), bf16[4,2,2,1,128,128]{5,4,2,1,3,0:T(8,128)(2,1)}, u32[]{:S(2)}, u32[]{:S(2)}) async-start(bf16[4,2,2,1,128,128]{5,4,2,1,3,0:T(8,128)(2,1)} %pad_maximum_fusion), calls=%async_computation | async-start | bytes 1048576 | tf_op jit(solution)/shard_map/all_to_all | solution.py:85
  42.6 19.1 %all-to-all-start.1 = ((bf16[2,2,4,128,128]{4,3,1,0,2:T(8,128)(2,1)}), bf16[2,2,4,128,128]{4,3,1,0,2:T(8,128)(2,1)}, u32[]{:S(2)}, u32[]{:S(2)}) async-start(bf16[2,2,4,128,128]{4,3,1,0,2:T(8,128)(2,1)} %select_bitcast_fusion), calls=%async_computation.1 | async-start | bytes 1048576 | tf_op jit(solution)/shard_map/all_to_all | solution.py:112
  61.7 58.6 %all-to-all-start.2 = ((bf16[2,2,4,128,128]{4,3,1,0,2:T(8,128)(2,1)}), bf16[2,2,4,128,128]{4,3,1,0,2:T(8,128)(2,1)}, u32[]{:S(2)}, u32[]{:S(2)}) async-start(bf16[2,2,4,128,128]{4,3,1,0,2:T(8,128)(2,1)} %select_bitcast_fusion.2), calls=%async_computation.2 | async-start | bytes 1048576 | tf_op jit(solution)/shard_map/all_to_all | solution.py:90
  71.5 8.7 %copy-start.4 = (bf16[1,2,4,1,128,128]{5,4,2,1,3,0:T(8,128)(2,1)S(1)}, bf16[1,2,4,1,128,128]{5,4,2,1,3,0:T(8,128)(2,1)}, u32[]{:S(2)}) copy-start(bf16[1,2,4,1,128,128]{5,4,2,1,3,0:T(8,128)(2,1)} %copy.23) | copy-start | bytes 786436
  80.1 10.7 %copy-start.6 = (bf16[2,512,128,1]{1,2,0,3:T(8,128)(2,1)S(1)}, bf16[2,512,128,1]{1,2,0,3:T(8,128)(2,1)}, u32[]{:S(2)}) copy-start(bf16[2,512,128,1]{1,2,0,3:T(8,128)(2,1)} %reshape.251) | copy-start | bytes 786436
  90.8 11.8 %copy-start.5 = (bf16[2,512,128,1]{1,2,0,3:T(8,128)(2,1)S(1)}, bf16[2,512,128,1]{1,2,0,3:T(8,128)(2,1)}, u32[]{:S(2)}) copy-start(bf16[2,512,128,1]{1,2,0,3:T(8,128)(2,1)} %reshape.249) | copy-start | bytes 786436
  98.8 9.4 %copy-start.3 = (bf16[2,2,512,128]{3,2,1,0:T(8,128)(2,1)S(1)}, bf16[2,2,512,128]{3,2,1,0:T(8,128)(2,1)}, u32[]{:S(2)}) copy-start(bf16[2,2,512,128]{3,2,1,0:T(8,128)(2,1)} %param.9) | copy-start | bytes 1572868
  108.1 14.9 %copy-start.1 = (s32[4,4,2]{1,2,0:T(2,128)S(1)}, s32[4,4,2]{1,2,0:T(2,128)}, u32[]{:S(2)}) copy-start(s32[4,4,2]{1,2,0:T(2,128)} %param.13) | copy-start | bytes 388
  122.1 1.0 copy-start.2
